TPU v7x, 128 devices: a whole 4x4x4 slice. The times are simulated.
128 devices in a mesh: row: 32 (over x, y, core), col: 4 (over z).
Axes of the slice: x: 4, y: 4, z: 4, core: 2. Of those that a mesh axis runs over, the one named last changes fastest.
Arguments:
- frames: float32 [64, 65536], P(None, ('row', 'col')), may hold values from -8 to 8
- start: float32 [32, 65536], P(None, ('row', 'col')), may hold values from -6 to 6
Outputs:
- basis: float32 [32, 65536], P(None, ('row', 'col'))
All inputs are finite; a program needn't handle non-finite values.
Results may differ from a plain program's by a relative error of at most 0.0003.
Values sent between devices are 32-bit elements; how exact they have to be, the bound alone decides.
A program may use at most 320 MiB of HBM per device.

v0:
```python
import jax
import jax.numpy as jnp
from jax import lax
from jax.sharding import PartitionSpec as P


def build_block(block_points, block_squares, column_points, column_squares):
    products = lax.dot_general(
        block_points, column_points, (((0,), (0,)), ((), ())), precision=lax.Precision.HIGHEST
    )
    distance = block_squares[:, None] + column_squares[None, :] - 2.0 * products
    return jnp.exp(-distance / (0.5 * block_points.shape[0]))


def shards(frames, start):
    block_points = lax.all_gather(frames, "col", axis=1, tiled=True)
    column_points = lax.all_gather(frames, "row", axis=1, tiled=True)
    block_squares = jnp.sum(block_points * block_points, axis=0)
    column_squares = jnp.sum(column_points * column_points, axis=0)
    frame_count = frames.shape[1] * lax.axis_size("row") * lax.axis_size("col")
    block_rows = block_points.shape[1]
    height = min(512, block_rows)
    rounds = block_rows // height

    def kernel_part(index):
        first = index * height
        return build_block(
            block_points[:, first : first + height],
            block_squares[first : first + height],
            column_points,
            column_squares,
        )

    stored = [kernel_part(index) for index in range(rounds)]

    def fetch_tile(index):
        return stored[index]

    def sweep_kernel(spread_weights):
        pieces = []
        for index in range(rounds):
            part = fetch_tile(index)
            if spread_weights is None:
                pieces.append(jnp.sum(part, axis=1)[None, :])
            else:
                pieces.append(
                    lax.dot_general(
                        spread_weights,
                        part,
                        (((1,), (1,)), ((), ())),
                        precision=lax.Precision.HIGHEST,
                    )
                )
        result = jnp.concatenate(pieces, axis=1)
        return result

    def settle(partial_value):
        summed = lax.psum_scatter(partial_value, "col", scatter_dimension=1, tiled=True)
        return summed

    def kernel_product(weights):
        spread_weights = lax.all_gather(weights, "row", axis=1, tiled=True)
        return settle(sweep_kernel(spread_weights))

    def gram_matrix(vectors):
        local_gram = jnp.dot(vectors, vectors.T, precision=lax.Precision.HIGHEST)
        return lax.psum(local_gram, ("row", "col")) / frame_count

    def orthonormal(vectors):
        factor = jnp.linalg.cholesky(gram_matrix(vectors))
        return jax.scipy.linalg.solve_triangular(factor, vectors, lower=True)

    density = settle(sweep_kernel(None))[0]
    inverse = 1.0 / density
    scaled = start * inverse[None, :]
    degree = kernel_product(inverse[None, :])[0]
    product = kernel_product(scaled)
    grown_one = product / degree[None, :]
    basis_one = orthonormal(grown_one)
    grown_two = kernel_product(basis_one * inverse[None, :]) / degree[None, :]
    return orthonormal(grown_two)


def solution(mesh):
    return jax.shard_map(
        shards,
        mesh=mesh,
        in_specs=(P(None, ("row", "col")), P(None, ("row", "col"))),
        out_specs=P(None, ("row", "col")),
        check_vma=False,
    )
```

profile of v0, /device:TPU:1, one launch (start us, length us, event | category | flops | bytes accessed | tf_op | source)
XLA Modules:
  0.0 895.1 jit_solution(2767273097480972749)
XLA Ops:
  6.5 0.7 all-gather.4.cloned.1.call-update
  7.3 0.0 reduce-scatter.13.cloned.1.call-start
  7.3 13.6 %all_gather.15 = f32[64,2048]{1,0:T(8,128)S(1)} all-gather(f32[64,512]{1,0:T(8,128)} %param.5), channel_id=1, replica_groups=mesh['row'=32,'col'=4] {'col'}, dimensions={1}, use_global_device_ids=true | all-gather | bytes 655360 | tf_op jit(solution)/shard_map/all_gather | solution.py:16
  20.9 0.1 multiply_reduce_fusion.1
  21.0 38.4 %all-gather.4.cloned.1.call-done = f32[64,16384]{1,0:T(8,128)} async-done(((f32[64,512]{1,0:T(8,128)}), f32[64,16384]{1,0:T(8,128)}) %all-gather.4.cloned.1.call-update) | async-done | bytes 4194320 | tf_op jit(solution)/shard_map/all_gather | solution.py:17
  59.3 2.7 multiply_reduce_fusion
  62.1 37.7 %fusion.27 = (f32[512]{0:T(512)S(1)}, f32[512,16384]{1,0:T(8,128)}) fusion(f32[64,16384]{1,0:T(8,128)} %all-gather.4.cloned.1.call-done, f32[64,2048]{1,0:T(8,128)S(1)} %all_gather.15, f32[16384]{0:T(1024)S(1)} %multiply_reduce_fusion, f32[512]{0:T(512)S(1)} %get-tuple-element.6), kind=kOutput, calls=%fused_computation.53 | convolution fusion | flops 6492782080 | bytes 37949440 | tf_op jit(solution)/shard_map/dot_general | solution.py:8
  99.8 37.0 %fusion.24 = (f32[512]{0:T(512)S(1)}, f32[512,16384]{1,0:T(8,128)}) fusion(f32[64,16384]{1,0:T(8,128)S(1)} %copy-done.2, f32[64,2048]{1,0:T(8,128)S(1)} %all_gather.15, f32[16384]{0:T(1024)S(1)} %multiply_reduce_fusion, f32[512]{0:T(512)S(1)} %get-tuple-element.8), kind=kOutput, calls=%fused_computation.50 | convolution fusion | flops 6492782080 | bytes 37949440 | tf_op jit(solution)/shard_map/dot_general | solution.py:8
  136.8 36.6 %fusion.25 = (f32[512]{0:T(512)S(1)}, f32[512,16384]{1,0:T(8,128)}) fusion(f32[64,16384]{1,0:T(8,128)S(1)} %copy-done.2, f32[64,2048]{1,0:T(8,128)S(1)} %all_gather.15, f32[16384]{0:T(1024)S(1)} %multiply_reduce_fusion, f32[512]{0:T(512)S(1)} %get-tuple-element.9), kind=kOutput, calls=%fused_computation.51 | convolution fusion | flops 6492782080 | bytes 37949440 | tf_op jit(solution)/shard_map/dot_general | solution.py:8
  173.4 36.7 %fusion.26 = (f32[512]{0:T(512)S(1)}, f32[512,16384]{1,0:T(8,128)}) fusion(f32[64,16384]{1,0:T(8,128)S(1)} %copy-done.2, f32[64,2048]{1,0:T(8,128)S(1)} %all_gather.15, f32[16384]{0:T(1024)S(1)} %multiply_reduce_fusion, f32[512]{0:T(512)S(1)} %get-tuple-element.10), kind=kOutput, calls=%fused_computation.52 | convolution fusion | flops 6492782080 | bytes 37949440 | tf_op jit(solution)/shard_map/dot_general | solution.py:8
  210.1 1.4 copy.13
  211.5 0.0 reduce-scatter.13.cloned.1.call-update
  211.5 0.0 all-gather.6.cloned.1.call-start
  211.6 21.5 %reduce-scatter.13.cloned.1.call-done = f32[512,1]{1,0:T(8,128)} async-done(((f32[2048,1]{1,0:T(8,128)}), f32[512,1]{1,0:T(8,128)}) %reduce-scatter.13.cloned.1.call-update) | async-done | bytes 2064
  233.0 1.1 copy.14
  234.1 26.0 %all_gather.18 = f32[1,16384]{1,0:T(1,128)S(1)} all-gather(f32[1,512]{1,0:T(1,128)S(1)} %broadcast_divide_fusion.6), channel_id=1, replica_groups=mesh['row'=32,'col'=4] {'row'}, dimensions={1}, use_global_device_ids=true | all-gather | bytes 67584 | tf_op jit(solution)/shard_map/all_gather | solution.py:62
  260.1 0.6 broadcast_multiply_fusion
  260.7 0.0 all-gather.6.cloned.1.call-update
  260.8 0.0 reduce-scatter.15.cloned.1.call-start
  260.8 31.2 %fusion.8 = f32[1,512]{1,0:T(1,128)S(1)} fusion(f32[512,16384]{1,0:T(8,128)} %get-tuple-element.16, f32[1,16384]{1,0:T(1,128)S(1)} %all_gather.18), kind=kOutput, calls=%fused_computation.17 | convolution fusion | flops 100663296 | bytes 33622016 | tf_op jit(solution)/shard_map/dot_general | solution.py:47
  292.0 30.9 %fusion.6 = f32[1,512]{1,0:T(1,128)S(1)} fusion(f32[512,16384]{1,0:T(8,128)} %get-tuple-element.14, f32[1,16384]{1,0:T(1,128)S(1)} %all_gather.18), kind=kOutput, calls=%fused_computation.15 | convolution fusion | flops 100663296 | bytes 33622016 | tf_op jit(solution)/shard_map/dot_general | solution.py:47
  322.9 31.0 %fusion.4 = f32[1,512]{1,0:T(1,128)S(1)} fusion(f32[512,16384]{1,0:T(8,128)} %get-tuple-element.12, f32[1,16384]{1,0:T(1,128)S(1)} %all_gather.18), kind=kOutput, calls=%fused_computation.13 | convolution fusion | flops 100663296 | bytes 33622016 | tf_op jit(solution)/shard_map/dot_general | solution.py:47
  353.9 30.8 %fusion.10 = f32[1,512]{1,0:T(1,128)S(1)} fusion(f32[512,16384]{1,0:T(8,128)} %get-tuple-element.18, f32[1,16384]{1,0:T(1,128)S(1)} %all_gather.18), kind=kOutput, calls=%fused_computation.19 | convolution fusion | flops 100663296 | bytes 33622016 | tf_op jit(solution)/shard_map/dot_general | solution.py:47
  384.7 1.4 copy.15
  386.0 0.0 reduce-scatter.15.cloned.1.call-update
  386.1 0.0 reduce-scatter.9.cloned.1.call-start
  386.1 0.0 all-gather.6.cloned.1.call-done
  386.2 34.4 %fusion.31 = f32[32,512]{1,0:T(8,128)S(1)} fusion(f32[32,16384]{1,0:T(8,128)} %all-gather.6.cloned.1.call-done, f32[512,16384]{1,0:T(8,128)} %get-tuple-element.12), kind=kOutput, calls=%fused_computation.57 | convolution fusion | flops 3221225472 | bytes 35717120 | tf_op jit(solution)/shard_map/dot_general | solution.py:47
  420.5 33.9 %fusion.30 = f32[32,512]{1,0:T(8,128)S(1)} fusion(f32[32,16384]{1,0:T(8,128)S(1)} %copy-done, f32[512,16384]{1,0:T(8,128)} %get-tuple-element.14), kind=kOutput, calls=%fused_computation.56 | convolution fusion | flops 3221225472 | bytes 35717120 | tf_op jit(solution)/shard_map/dot_general | solution.py:47
  454.4 34.3 %fusion.29 = f32[32,512]{1,0:T(8,128)S(1)} fusion(f32[32,16384]{1,0:T(8,128)S(1)} %copy-done, f32[512,16384]{1,0:T(8,128)} %get-tuple-element.16), kind=kOutput, calls=%fused_computation.55 | convolution fusion | flops 3221225472 | bytes 35717120 | tf_op jit(solution)/shard_map/dot_general | solution.py:47
  488.8 33.9 %fusion.28 = f32[32,512]{1,0:T(8,128)S(1)} fusion(f32[32,16384]{1,0:T(8,128)S(1)} %copy-done, f32[512,16384]{1,0:T(8,128)} %get-tuple-element.18), kind=kOutput, calls=%fused_computation.54 | convolution fusion | flops 3221225472 | bytes 35717120 | tf_op jit(solution)/shard_map/dot_general | solution.py:47
  522.6 0.7 pad_maximum_fusion
  523.3 0.0 reduce-scatter.9.cloned.1.call-update
  523.4 0.0 all-gather.8.cloned.1.call-start
  523.4 0.0 reduce-scatter.15.cloned.1.call-done
  523.4 1.1 copy.16
  524.5 14.8 %reduce-scatter.9.cloned.1.call-done = f32[32,512]{1,0:T(8,128)} async-done(((f32[32,2048]{1,0:T(8,128)}), f32[32,512]{1,0:T(8,128)}) %reduce-scatter.9.cloned.1.call-update) | async-done | bytes 65552 | tf_op jit(solution)/shard_map/reduce_scatter | solution.py:58
  539.3 1.1 fusion.12
  540.4 67.2 %psum.14 = f32[32,32]{0,1:T(8,128)S(1)} all-reduce(f32[32,32]{0,1:T(8,128)S(1)} %fusion.12), channel_id=1, replica_groups=mesh['row'=32,'col'=4] {'row','col'}, use_global_device_ids=true, to_apply=%region_9.0 | all-reduce | flops 1024 | bytes 8192 | tf_op jit(solution)/shard_map/psum | solution.py:67
  607.6 0.1 copy.8
  607.7 2.9 cholesky.44
  610.6 0.6 compare_reduce_fusion.1
  611.3 0.7 fusion.15
  611.9 2.4 custom-call.6
  614.4 1.8 convolution_multiply_fusion
  616.1 0.0 all-gather.8.cloned.1.call-update
  616.1 0.0 reduce-scatter.11.cloned.1.call-start
  616.2 40.7 %all-gather.8.cloned.1.call-done = f32[32,16384]{1,0:T(8,128)} async-done(((f32[32,512]{1,0:T(8,128)}), f32[32,16384]{1,0:T(8,128)}) %all-gather.8.cloned.1.call-update) | async-done | bytes 2097168 | tf_op jit(solution)/shard_map/all_gather | solution.py:62
  656.8 34.2 %fusion.35 = f32[32,512]{1,0:T(8,128)S(1)} fusion(f32[32,16384]{1,0:T(8,128)} %all-gather.8.cloned.1.call-done, f32[512,16384]{1,0:T(8,128)} %get-tuple-element.12), kind=kOutput, calls=%fused_computation.61 | convolution fusion | flops 3221225472 | bytes 35717120 | tf_op jit(solution)/shard_map/dot_general | solution.py:47
  691.0 0.0 copy-done.1
  691.0 33.9 %fusion.34 = f32[32,512]{1,0:T(8,128)S(1)} fusion(f32[32,16384]{1,0:T(8,128)S(1)} %copy-done.1, f32[512,16384]{1,0:T(8,128)} %get-tuple-element.14), kind=kOutput, calls=%fused_computation.60 | convolution fusion | flops 3221225472 | bytes 35717120 | tf_op jit(solution)/shard_map/dot_general | solution.py:47
  724.9 34.1 %fusion.33 = f32[32,512]{1,0:T(8,128)S(1)} fusion(f32[32,16384]{1,0:T(8,128)S(1)} %copy-done.1, f32[512,16384]{1,0:T(8,128)} %get-tuple-element.16), kind=kOutput, calls=%fused_computation.59 | convolution fusion | flops 3221225472 | bytes 35717120 | tf_op jit(solution)/shard_map/dot_general | solution.py:47
  759.0 33.9 %fusion.32 = f32[32,512]{1,0:T(8,128)S(1)} fusion(f32[32,16384]{1,0:T(8,128)S(1)} %copy-done.1, f32[512,16384]{1,0:T(8,128)} %get-tuple-element.18), kind=kOutput, calls=%fused_computation.58 | convolution fusion | flops 3221225472 | bytes 35717120 | tf_op jit(solution)/shard_map/dot_general | solution.py:47
  792.9 0.7 pad_maximum_fusion.1
  793.6 0.0 reduce-scatter.11.cloned.1.call-update
  793.6 17.6 %reduce-scatter.11.cloned.1.call-done = f32[32,512]{1,0:T(8,128)} async-done(((f32[32,2048]{1,0:T(8,128)}), f32[32,512]{1,0:T(8,128)}) %reduce-scatter.11.cloned.1.call-update) | async-done | bytes 65552 | tf_op jit(solution)/shard_map/reduce_scatter | solution.py:58
  811.2 1.1 fusion.14
  812.3 67.0 %psum.15 = f32[32,32]{0,1:T(8,128)S(1)} all-reduce(f32[32,32]{0,1:T(8,128)S(1)} %fusion.14), channel_id=1, replica_groups=mesh['row'=32,'col'=4] {'row','col'}, use_global_device_ids=true, to_apply=%region_13.16 | all-reduce | flops 1024 | bytes 8192 | tf_op jit(solution)/shard_map/psum | solution.py:67
  879.3 0.1 copy.10
  879.4 2.9 cholesky.55
  882.4 0.6 compare_reduce_fusion
  883.0 0.7 fusion.16
  883.7 2.4 custom-call.7
  886.1 1.8 fusion.13
  (18 shorter events, 0.1 us)
Async XLA Ops:
  6.5 52.8 %all-gather.4.cloned.1.call-start = ((), (), s32[]{:S(2)}) async-start(), calls=%async_computation.4 | async-start | bytes 4325376 | tf_op jit(solution)/shard_map/all_gather | solution.py:17
  7.3 225.8 %reduce-scatter.13.cloned.1.call-start = ((), (), s32[]{:S(2)}) async-start(), calls=%async_computation.9 | async-start | bytes 1310720
  59.3 40.5 %copy-start.2 = (f32[64,16384]{1,0:T(8,128)S(1)}, f32[64,16384]{1,0:T(8,128)}, u32[]{:S(2)}) copy-start(f32[64,16384]{1,0:T(8,128)} %all-gather.4.cloned.1.call-done) | copy-start | bytes 12582916
  173.4 86.7 %copy-start.3 = (f32[32,512]{1,0:T(8,128)S(1)}, f32[32,512]{1,0:T(8,128)}, u32[]{:S(2)}) copy-start(f32[32,512]{1,0:T(8,128)} %param.6) | copy-start | bytes 196612
  211.5 174.6 %all-gather.6.cloned.1.call-start = ((), (), s32[]{:S(2)}) async-start(), calls=%async_computation.5 | async-start | bytes 2162688 | tf_op jit(solution)/shard_map/all_gather | solution.py:62
  260.8 262.7 %reduce-scatter.15.cloned.1.call-start = ((), (), s32[]{:S(2)}) async-start(), calls=%async_computation.10 | async-start | bytes 1310720
  386.1 153.2 %reduce-scatter.9.cloned.1.call-start = ((), (), s32[]{:S(2)}) async-start(), calls=%async_computation.6 | async-start | bytes 327680 | tf_op jit(solution)/shard_map/reduce_scatter | solution.py:58
  386.1 34.4 %copy-start = (f32[32,16384]{1,0:T(8,128)S(1)}, f32[32,16384]{1,0:T(8,128)}, u32[]{:S(2)}) copy-start(f32[32,16384]{1,0:T(8,128)} %all-gather.6.cloned.1.call-done) | copy-start | bytes 6291460
  523.4 133.5 %all-gather.8.cloned.1.call-start = ((), (), s32[]{:S(2)}) async-start(), calls=%async_computation.7 | async-start | bytes 2162688 | tf_op jit(solution)/shard_map/all_gather | solution.py:62
  616.1 195.1 %reduce-scatter.11.cloned.1.call-start = ((), (), s32[]{:S(2)}) async-start(), calls=%async_computation.8 | async-start | bytes 327680 | tf_op jit(solution)/shard_map/reduce_scatter | solution.py:58
  656.8 34.2 %copy-start.1 = (f32[32,16384]{1,0:T(8,128)S(1)}, f32[32,16384]{1,0:T(8,128)}, u32[]{:S(2)}) copy-start(f32[32,16384]{1,0:T(8,128)} %all-gather.8.cloned.1.call-done) | copy-start | bytes 6291460
Sparse Core Ops, SparseCore 0:
  9.7 49.5 all-gather.3
  211.6 21.3 reduce-scatter.12
  260.9 41.3 all-gather.5
  386.2 19.1 reduce-scatter.14
  523.5 15.7 reduce-scatter.8
  616.3 40.5 all-gather.7
  793.7 17.4 reduce-scatter.10
where the time goes:
time: 902 us; the launch traced here: 895 us
  matrix products  550 us (61%)
  blocking collectives  174 us (19%)
  waiting for transfers between devices  134 us (15%)
  other arithmetic  18.3 us (2%)
  between operations  14 us (2%)
    dot_general x12, matrix products, sweep_kernel(): lax.dot_general(spread_weights, part, (((1,), (1,)), ((), ())), precision...  396 us
    dot_general x4, matrix products, build_block(): lax.dot_general(block_points, column_points, (((0,), (0,)), ((), ())), pr...  148 us
    psum x2, blocking collectives, gram_matrix(): return lax.psum(local_gram, ('row', 'col')) / frame_count  134 us
    all_gather x2, waiting for transfers between devices, kernel_product(): spread_weights = lax.all_gather(weights, 'row', axis=1, tiled=True)  40.7 us
    all_gather x1, waiting for transfers between devices, shards(): column_points = lax.all_gather(frames, 'row', axis=1, tiled=True)  38.4 us
    reduce_scatter x2, waiting for transfers between devices, settle(): lax.psum_scatter(partial_value, 'col', scatter_dimension=1, tiled=True)  32.4 us
    all_gather x1, blocking collectives, kernel_product(): spread_weights = lax.all_gather(weights, 'row', axis=1, tiled=True)  26 us
    unnamed x9, waiting for transfers between devices  22.3 us
  transfers between devices with their start and end apart: 7, of which 5 were waited for; matrix products, arithmetic and copies ran while one was open for 29% of the time, Pallas kernels for 0%

commit v1 on v0

--- a/solution.py
+++ b/solution.py
@@ -2,6 +2,11 @@
 import jax.numpy as jnp
 from jax import lax
 from jax.sharding import PartitionSpec as P
+
+
+def one_after_other(value, inner_axis, outer_axis):
+    half = lax.psum(value, inner_axis)
+    return lax.psum(half, outer_axis)
 
 
 def build_block(block_points, block_squares, column_points, column_squares):
@@ -64,7 +69,7 @@
 
     def gram_matrix(vectors):
         local_gram = jnp.dot(vectors, vectors.T, precision=lax.Precision.HIGHEST)
-        return lax.psum(local_gram, ("row", "col")) / frame_count
+        return one_after_other(local_gram, "col", "row") / frame_count
 
     def orthonormal(vectors):
         factor = jnp.linalg.cholesky(gram_matrix(vectors))

time: 902 us -> 1050 us (1.16)
  blocking collectives: 174 us -> 312 us
    psum x2 -> x4, blocking collectives: 134 us -> 272 us  [the longest x2 248 us: one_after_other(): return lax.psum(half, outer_axis)]
  transfers between devices with their start and end apart: 7 -> 7, of which waited for: 5 -> 5; matrix products, arithmetic and copies ran while one was open for 29% -> 25% of each run, Pallas kernels for 0% -> 0%
where the time goes in v1:
time: 1050 us; the launch traced here: 1040 us
  matrix products  550 us (52%)
  blocking collectives  312 us (30%)
  waiting for transfers between devices  136 us (13%)
  other arithmetic  18.3 us (2%)
  between operations  13.9 us (1%)
    dot_general x12, matrix products, sweep_kernel(): lax.dot_general(spread_weights, part, (((1,), (1,)), ((), ())), precision...  396 us
    psum x2, blocking collectives, one_after_other(): return lax.psum(half, outer_axis)  248 us
    dot_general x4, matrix products, build_block(): lax.dot_general(block_points, column_points, (((0,), (0,)), ((), ())), pr...  148 us
    all_gather x2, waiting for transfers between devices, kernel_product(): spread_weights = lax.all_gather(weights, 'row', axis=1, tiled=True)  43.4 us
    all_gather x1, waiting for transfers between devices, shards(): column_points = lax.all_gather(frames, 'row', axis=1, tiled=True)  38.4 us
    reduce_scatter x2, waiting for transfers between devices, settle(): lax.psum_scatter(partial_value, 'col', scatter_dimension=1, tiled=True)  32.4 us
    all_gather x1, blocking collectives, kernel_product(): spread_weights = lax.all_gather(weights, 'row', axis=1, tiled=True)  26 us
    psum x2, blocking collectives, one_after_other(): half = lax.psum(value, inner_axis)  23.7 us
  transfers between devices with their start and end apart: 7, of which 5 were waited for; matrix products, arithmetic and copies ran while one was open for 25% of the time, Pallas kernels for 0%

profile of v1, /device:TPU:1, one launch (start us, length us, event | category | flops | bytes accessed | tf_op | source)
XLA Modules:
  0.0 1035.5 jit_solution(16084491066478499335)
XLA Ops:
  6.5 0.7 all-gather.4.cloned.1.call-update
  7.3 0.0 reduce-scatter.13.cloned.1.call-start
  7.3 13.6 %all_gather.15 = f32[64,2048]{1,0:T(8,128)S(1)} all-gather(f32[64,512]{1,0:T(8,128)} %param.5), channel_id=1, replica_groups=mesh['row'=32,'col'=4] {'col'}, dimensions={1}, use_global_device_ids=true | all-gather | bytes 655360 | tf_op jit(solution)/shard_map/all_gather | solution.py:21
  20.9 0.1 multiply_reduce_fusion.1
  21.0 38.4 %all-gather.4.cloned.1.call-done = f32[64,16384]{1,0:T(8,128)} async-done(((f32[64,512]{1,0:T(8,128)}), f32[64,16384]{1,0:T(8,128)}) %all-gather.4.cloned.1.call-update) | async-done | bytes 4194320 | tf_op jit(solution)/shard_map/all_gather | solution.py:22
  59.3 2.7 multiply_reduce_fusion
  62.1 37.7 %fusion.27 = (f32[512]{0:T(512)S(1)}, f32[512,16384]{1,0:T(8,128)}) fusion(f32[64,16384]{1,0:T(8,128)} %all-gather.4.cloned.1.call-done, f32[64,2048]{1,0:T(8,128)S(1)} %all_gather.15, f32[16384]{0:T(1024)S(1)} %multiply_reduce_fusion, f32[512]{0:T(512)S(1)} %get-tuple-element.6), kind=kOutput, calls=%fused_computation.53 | convolution fusion | flops 6492782080 | bytes 37949440 | tf_op jit(solution)/shard_map/dot_general | solution.py:13
  99.8 37.0 %fusion.24 = (f32[512]{0:T(512)S(1)}, f32[512,16384]{1,0:T(8,128)}) fusion(f32[64,16384]{1,0:T(8,128)S(1)} %copy-done.2, f32[64,2048]{1,0:T(8,128)S(1)} %all_gather.15, f32[16384]{0:T(1024)S(1)} %multiply_reduce_fusion, f32[512]{0:T(512)S(1)} %get-tuple-element.8), kind=kOutput, calls=%fused_computation.50 | convolution fusion | flops 6492782080 | bytes 37949440 | tf_op jit(solution)/shard_map/dot_general | solution.py:13
  136.8 36.6 %fusion.25 = (f32[512]{0:T(512)S(1)}, f32[512,16384]{1,0:T(8,128)}) fusion(f32[64,16384]{1,0:T(8,128)S(1)} %copy-done.2, f32[64,2048]{1,0:T(8,128)S(1)} %all_gather.15, f32[16384]{0:T(1024)S(1)} %multiply_reduce_fusion, f32[512]{0:T(512)S(1)} %get-tuple-element.9), kind=kOutput, calls=%fused_computation.51 | convolution fusion | flops 6492782080 | bytes 37949440 | tf_op jit(solution)/shard_map/dot_general | solution.py:13
  173.4 36.7 %fusion.26 = (f32[512]{0:T(512)S(1)}, f32[512,16384]{1,0:T(8,128)}) fusion(f32[64,16384]{1,0:T(8,128)S(1)} %copy-done.2, f32[64,2048]{1,0:T(8,128)S(1)} %all_gather.15, f32[16384]{0:T(1024)S(1)} %multiply_reduce_fusion, f32[512]{0:T(512)S(1)} %get-tuple-element.10), kind=kOutput, calls=%fused_computation.52 | convolution fusion | flops 6492782080 | bytes 37949440 | tf_op jit(solution)/shard_map/dot_general | solution.py:13
  210.1 1.4 copy.13
  211.5 0.0 reduce-scatter.13.cloned.1.call-update
  211.5 0.0 all-gather.6.cloned.1.call-start
  211.6 21.5 %reduce-scatter.13.cloned.1.call-done = f32[512,1]{1,0:T(8,128)} async-done(((f32[2048,1]{1,0:T(8,128)}), f32[512,1]{1,0:T(8,128)}) %reduce-scatter.13.cloned.1.call-update) | async-done | bytes 2064
  233.0 1.1 copy.14
  234.1 26.0 %all_gather.18 = f32[1,16384]{1,0:T(1,128)S(1)} all-gather(f32[1,512]{1,0:T(1,128)S(1)} %broadcast_divide_fusion.6), channel_id=1, replica_groups=mesh['row'=32,'col'=4] {'row'}, dimensions={1}, use_global_device_ids=true | all-gather | bytes 67584 | tf_op jit(solution)/shard_map/all_gather | solution.py:67
  260.1 0.6 broadcast_multiply_fusion
  260.7 0.0 all-gather.6.cloned.1.call-update
  260.8 0.0 reduce-scatter.15.cloned.1.call-start
  260.8 31.2 %fusion.8 = f32[1,512]{1,0:T(1,128)S(1)} fusion(f32[512,16384]{1,0:T(8,128)} %get-tuple-element.16, f32[1,16384]{1,0:T(1,128)S(1)} %all_gather.18), kind=kOutput, calls=%fused_computation.17 | convolution fusion | flops 100663296 | bytes 33622016 | tf_op jit(solution)/shard_map/dot_general | solution.py:52
  292.0 30.9 %fusion.6 = f32[1,512]{1,0:T(1,128)S(1)} fusion(f32[512,16384]{1,0:T(8,128)} %get-tuple-element.14, f32[1,16384]{1,0:T(1,128)S(1)} %all_gather.18), kind=kOutput, calls=%fused_computation.15 | convolution fusion | flops 100663296 | bytes 33622016 | tf_op jit(solution)/shard_map/dot_general | solution.py:52
  322.9 31.0 %fusion.4 = f32[1,512]{1,0:T(1,128)S(1)} fusion(f32[512,16384]{1,0:T(8,128)} %get-tuple-element.12, f32[1,16384]{1,0:T(1,128)S(1)} %all_gather.18), kind=kOutput, calls=%fused_computation.13 | convolution fusion | flops 100663296 | bytes 33622016 | tf_op jit(solution)/shard_map/dot_general | solution.py:52
  353.9 30.8 %fusion.10 = f32[1,512]{1,0:T(1,128)S(1)} fusion(f32[512,16384]{1,0:T(8,128)} %get-tuple-element.18, f32[1,16384]{1,0:T(1,128)S(1)} %all_gather.18), kind=kOutput, calls=%fused_computation.19 | convolution fusion | flops 100663296 | bytes 33622016 | tf_op jit(solution)/shard_map/dot_general | solution.py:52
  384.7 1.4 copy.15
  386.0 0.0 reduce-scatter.15.cloned.1.call-update
  386.1 0.0 reduce-scatter.9.cloned.1.call-start
  386.1 0.0 all-gather.6.cloned.1.call-done
  386.2 34.4 %fusion.31 = f32[32,512]{1,0:T(8,128)S(1)} fusion(f32[32,16384]{1,0:T(8,128)} %all-gather.6.cloned.1.call-done, f32[512,16384]{1,0:T(8,128)} %get-tuple-element.12), kind=kOutput, calls=%fused_computation.57 | convolution fusion | flops 3221225472 | bytes 35717120 | tf_op jit(solution)/shard_map/dot_general | solution.py:52
  420.5 33.9 %fusion.30 = f32[32,512]{1,0:T(8,128)S(1)} fusion(f32[32,16384]{1,0:T(8,128)S(1)} %copy-done, f32[512,16384]{1,0:T(8,128)} %get-tuple-element.14), kind=kOutput, calls=%fused_computation.56 | convolution fusion | flops 3221225472 | bytes 35717120 | tf_op jit(solution)/shard_map/dot_general | solution.py:52
  454.4 34.3 %fusion.29 = f32[32,512]{1,0:T(8,128)S(1)} fusion(f32[32,16384]{1,0:T(8,128)S(1)} %copy-done, f32[512,16384]{1,0:T(8,128)} %get-tuple-element.16), kind=kOutput, calls=%fused_computation.55 | convolution fusion | flops 3221225472 | bytes 35717120 | tf_op jit(solution)/shard_map/dot_general | solution.py:52
  488.8 33.9 %fusion.28 = f32[32,512]{1,0:T(8,128)S(1)} fusion(f32[32,16384]{1,0:T(8,128)S(1)} %copy-done, f32[512,16384]{1,0:T(8,128)} %get-tuple-element.18), kind=kOutput, calls=%fused_computation.54 | convolution fusion | flops 3221225472 | bytes 35717120 | tf_op jit(solution)/shard_map/dot_general | solution.py:52
  522.6 0.7 pad_maximum_fusion
  523.3 0.0 reduce-scatter.9.cloned.1.call-update
  523.4 0.0 all-gather.8.cloned.1.call-start
  523.4 0.0 reduce-scatter.15.cloned.1.call-done
  523.4 1.1 copy.16
  524.5 14.8 %reduce-scatter.9.cloned.1.call-done = f32[32,512]{1,0:T(8,128)} async-done(((f32[32,2048]{1,0:T(8,128)}), f32[32,512]{1,0:T(8,128)}) %reduce-scatter.9.cloned.1.call-update) | async-done | bytes 65552 | tf_op jit(solution)/shard_map/reduce_scatter | solution.py:63
  539.3 1.1 fusion.12
  540.4 12.0 %psum.28 = f32[32,32]{0,1:T(8,128)S(1)} all-reduce(f32[32,32]{0,1:T(8,128)S(1)} %fusion.12), channel_id=1, replica_groups=mesh['row'=32,'col'=4] {'col'}, use_global_device_ids=true, to_apply=%region_9.0 | all-reduce | flops 1024 | bytes 8192 | tf_op jit(solution)/shard_map/psum | solution.py:8
  552.4 124.2 %psum.29 = f32[32,32]{0,1:T(8,128)S(1)} all-reduce(f32[32,32]{0,1:T(8,128)S(1)} %psum.28), channel_id=1, replica_groups=mesh['row'=32,'col'=4] {'row'}, use_global_device_ids=true, to_apply=%region_10.0 | all-reduce | flops 1024 | bytes 8192 | tf_op jit(solution)/shard_map/psum | solution.py:9
  676.6 0.1 copy.8
  676.7 2.9 cholesky.44
  679.6 0.6 compare_reduce_fusion.1
  680.3 0.7 fusion.15
  680.9 2.4 custom-call.6
  683.4 1.8 convolution_multiply_fusion
  685.1 0.0 reduce-scatter.11.cloned.1.call-start
  685.2 43.3 %all-gather.8.cloned.1.call-done = f32[32,16384]{1,0:T(8,128)} async-done(((f32[32,512]{1,0:T(8,128)}), f32[32,16384]{1,0:T(8,128)}) %all-gather.8.cloned.1.call-update) | async-done | bytes 2097168 | tf_op jit(solution)/shard_map/all_gather | solution.py:67
  728.5 34.2 %fusion.35 = f32[32,512]{1,0:T(8,128)S(1)} fusion(f32[32,16384]{1,0:T(8,128)} %all-gather.8.cloned.1.call-done, f32[512,16384]{1,0:T(8,128)} %get-tuple-element.12), kind=kOutput, calls=%fused_computation.61 | convolution fusion | flops 3221225472 | bytes 35717120 | tf_op jit(solution)/shard_map/dot_general | solution.py:52
  762.7 33.9 %fusion.34 = f32[32,512]{1,0:T(8,128)S(1)} fusion(f32[32,16384]{1,0:T(8,128)S(1)} %copy-done.1, f32[512,16384]{1,0:T(8,128)} %get-tuple-element.14), kind=kOutput, calls=%fused_computation.60 | convolution fusion | flops 3221225472 | bytes 35717120 | tf_op jit(solution)/shard_map/dot_general | solution.py:52
  796.6 34.1 %fusion.33 = f32[32,512]{1,0:T(8,128)S(1)} fusion(f32[32,16384]{1,0:T(8,128)S(1)} %copy-done.1, f32[512,16384]{1,0:T(8,128)} %get-tuple-element.16), kind=kOutput, calls=%fused_computation.59 | convolution fusion | flops 3221225472 | bytes 35717120 | tf_op jit(solution)/shard_map/dot_general | solution.py:52
  830.7 33.9 %fusion.32 = f32[32,512]{1,0:T(8,128)S(1)} fusion(f32[32,16384]{1,0:T(8,128)S(1)} %copy-done.1, f32[512,16384]{1,0:T(8,128)} %get-tuple-element.18), kind=kOutput, calls=%fused_computation.58 | convolution fusion | flops 3221225472 | bytes 35717120 | tf_op jit(solution)/shard_map/dot_general | solution.py:52
  864.6 0.7 pad_maximum_fusion.1
  865.3 0.0 reduce-scatter.11.cloned.1.call-update
  865.3 17.6 %reduce-scatter.11.cloned.1.call-done = f32[32,512]{1,0:T(8,128)} async-done(((f32[32,2048]{1,0:T(8,128)}), f32[32,512]{1,0:T(8,128)}) %reduce-scatter.11.cloned.1.call-update) | async-done | bytes 65552 | tf_op jit(solution)/shard_map/reduce_scatter | solution.py:63
  882.9 1.1 fusion.14
  884.0 11.7 %psum.30 = f32[32,32]{0,1:T(8,128)S(1)} all-reduce(f32[32,32]{0,1:T(8,128)S(1)} %fusion.14), channel_id=1, replica_groups=mesh['row'=32,'col'=4] {'col'}, use_global_device_ids=true, to_apply=%region_14.17 | all-reduce | flops 1024 | bytes 8192 | tf_op jit(solution)/shard_map/psum | solution.py:8
  895.8 124.2 %psum.31 = f32[32,32]{0,1:T(8,128)S(1)} all-reduce(f32[32,32]{0,1:T(8,128)S(1)} %psum.30), channel_id=1, replica_groups=mesh['row'=32,'col'=4] {'row'}, use_global_device_ids=true, to_apply=%region_15.18 | all-reduce | flops 1024 | bytes 8192 | tf_op jit(solution)/shard_map/psum | solution.py:9
  1019.9 0.1 copy.10
  1020.0 2.9 cholesky.55
  1023.0 0.6 compare_reduce_fusion
  1023.6 0.7 fusion.16
  1024.3 2.4 custom-call.7
  1026.7 1.8 fusion.13
  (20 shorter events, 0.2 us)
Async XLA Ops:
  6.5 52.8 %all-gather.4.cloned.1.call-start = ((), (), s32[]{:S(2)}) async-start(), calls=%async_computation.4 | async-start | bytes 4325376 | tf_op jit(solution)/shard_map/all_gather | solution.py:22
  7.3 225.8 %reduce-scatter.13.cloned.1.call-start = ((), (), s32[]{:S(2)}) async-start(), calls=%async_computation.9 | async-start | bytes 1310720
  59.3 40.5 %copy-start.2 = (f32[64,16384]{1,0:T(8,128)S(1)}, f32[64,16384]{1,0:T(8,128)}, u32[]{:S(2)}) copy-start(f32[64,16384]{1,0:T(8,128)} %all-gather.4.cloned.1.call-done) | copy-start | bytes 12582916
  173.4 86.7 %copy-start.3 = (f32[32,512]{1,0:T(8,128)S(1)}, f32[32,512]{1,0:T(8,128)}, u32[]{:S(2)}) copy-start(f32[32,512]{1,0:T(8,128)} %param.6) | copy-start | bytes 196612
  211.5 174.6 %all-gather.6.cloned.1.call-start = ((), (), s32[]{:S(2)}) async-start(), calls=%async_computation.5 | async-start | bytes 2162688 | tf_op jit(solution)/shard_map/all_gather | solution.py:67
  260.8 262.7 %reduce-scatter.15.cloned.1.call-start = ((), (), s32[]{:S(2)}) async-start(), calls=%async_computation.10 | async-start | bytes 1310720
  386.1 153.2 %reduce-scatter.9.cloned.1.call-start = ((), (), s32[]{:S(2)}) async-start(), calls=%async_computation.6 | async-start | bytes 327680 | tf_op jit(solution)/shard_map/reduce_scatter | solution.py:63
  386.1 34.4 %copy-start = (f32[32,16384]{1,0:T(8,128)S(1)}, f32[32,16384]{1,0:T(8,128)}, u32[]{:S(2)}) copy-start(f32[32,16384]{1,0:T(8,128)} %all-gather.6.cloned.1.call-done) | copy-start | bytes 6291460
  523.4 205.2 %all-gather.8.cloned.1.call-start = ((), (), s32[]{:S(2)}) async-start(), calls=%async_computation.7 | async-start | bytes 2162688 | tf_op jit(solution)/shard_map/all_gather | solution.py:67
  685.1 197.8 %reduce-scatter.11.cloned.1.call-start = ((), (), s32[]{:S(2)}) async-start(), calls=%async_computation.8 | async-start | bytes 327680 | tf_op jit(solution)/shard_map/reduce_scatter | solution.py:63
  728.5 34.2 %copy-start.1 = (f32[32,16384]{1,0:T(8,128)S(1)}, f32[32,16384]{1,0:T(8,128)}, u32[]{:S(2)}) copy-start(f32[32,16384]{1,0:T(8,128)} %all-gather.8.cloned.1.call-done) | copy-start | bytes 6291460
Sparse Core Ops, SparseCore 0:
  9.7 49.5 all-gather.3
  211.6 21.3 reduce-scatter.12
  260.9 41.3 all-gather.5
  386.2 19.1 reduce-scatter.14
  523.5 15.7 reduce-scatter.8
  685.3 43.2 all-gather.7
  865.4 17.4 reduce-scatter.10
